TPU v7x, 256 devices: a whole 4x4x8 slice. The times are simulated.
256 devices in a mesh: row: 4 (over y_lo, core), col: 64 (over x, y_hi, z).
Axes of the slice: x: 4, y: 4 (y_hi: 2, y_lo: 2; y = y_hi * 2 + y_lo), z: 8, core: 2. Of those that a mesh axis runs over, the one named last changes fastest.
Arguments:
- tensor: bfloat16 [128, 3072, 4096], P(None, 'col', 'row'), may hold values from -6 to 6
- first_factor: bfloat16 [64, 4096], P(None, ('row', 'col')), may hold values from -0.453125 to 0.453125
- second_factor: bfloat16 [64, 3072], P(None, 'col'), may hold values from -0.5232237 to 0.5232237
Outputs:
- frames: float32 [64, 128], replicated
- mode_one: float32 [64, 4096], P(None, ('row', 'col'))
All inputs are finite; a program needn't handle non-finite values.
Results may differ from a plain program's by a relative error of at most 0.004.
Values may be sent and summed in bfloat16 or wider, within the bound.
A program may use at most 128 MiB of HBM per device.

v0:
```python
import functools

import jax
import jax.numpy as jnp
from jax import lax
from jax.experimental import pallas as pl
from jax.experimental.pallas import tpu as pltpu
from jax.sharding import PartitionSpec as P

ridge_weight = 0.05
MESH_ID = pl.DeviceIdType.MESH


def ridge_solve(gram, right_side):
    order_size = gram.shape[0]
    factor_low = jnp.linalg.cholesky(gram + ridge_weight * jnp.eye(order_size, dtype=jnp.float32))
    middle = lax.linalg.triangular_solve(factor_low, right_side, left_side=True, lower=True)
    return lax.linalg.triangular_solve(
        factor_low, middle, left_side=True, lower=True, transpose_a=True
    )


def gram_of(factor):
    return jnp.dot(factor, factor.T, preferred_element_type=jnp.float32)


STREAM_ROWS = 768


def _project_kernel(portion_ref, slab_ref, out_ref):
    out_ref[...] = lax.dot_general(
        portion_ref[...], slab_ref[...], (((1,), (1,)), ((), ())),
        preferred_element_type=jnp.float32,
    )


def project_columns(flattened, portion):
    cols, rows = flattened.shape
    components = portion.shape[0]
    return pl.pallas_call(
        _project_kernel,
        grid=(cols // STREAM_ROWS,),
        in_specs=[
            pl.BlockSpec((components, rows), lambda s: (0, 0)),
            pl.BlockSpec((STREAM_ROWS, rows), lambda s: (s, 0)),
        ],
        out_specs=pl.BlockSpec((components, STREAM_ROWS), lambda s: (0, s)),
        out_shape=jax.ShapeDtypeStruct((components, cols), jnp.float32),
        cost_estimate=pl.CostEstimate(
            flops=2 * components * cols * rows, transcendentals=0,
            bytes_accessed=2 * cols * rows + 4 * components * cols,
        ),
    )(portion, flattened)


def _accumulate_kernel(weights_ref, slab_ref, out_ref):
    @pl.when(pl.program_id(0) == 0)
    def _():
        out_ref[...] = jnp.zeros_like(out_ref)

    out_ref[...] += jnp.dot(weights_ref[...], slab_ref[...], preferred_element_type=jnp.float32)


def accumulate_rows(weights, flattened):
    cols, rows = flattened.shape
    components = weights.shape[0]
    return pl.pallas_call(
        _accumulate_kernel,
        grid=(cols // STREAM_ROWS,),
        in_specs=[
            pl.BlockSpec((components, STREAM_ROWS), lambda s: (0, s)),
            pl.BlockSpec((STREAM_ROWS, rows), lambda s: (s, 0)),
        ],
        out_specs=pl.BlockSpec((components, rows), lambda s: (0, 0)),
        out_shape=jax.ShapeDtypeStruct((components, rows), jnp.float32),
        cost_estimate=pl.CostEstimate(
            flops=2 * components * cols * rows, transcendentals=0,
            bytes_accessed=2 * cols * rows + 2 * components * cols,
        ),
    )(weights, flattened)


def spread_product(frames, second):
    product = frames[:, :, None] * second[:, None, :]
    return product.astype(jnp.bfloat16).reshape(frames.shape[0], -1)


def _exchange_kernel(n, mode, send_ref, out_ref, recv, send_sems, recv_sems, *extra):
    me = lax.axis_index("col")
    row = lax.axis_index("row")
    broadcast = mode == "gather"

    def exchange(source, landing, sends, recvs):
        def descriptor(peer, slot):
            return pltpu.make_async_remote_copy(
                src_ref=source(peer),
                dst_ref=landing.at[slot],
                send_sem=sends.at[peer],
                recv_sem=recvs.at[slot],
                device_id=(row, peer),
                device_id_type=MESH_ID,
            )

        def start(t, carry):
            peer = lax.rem(me + 1 + t, n)
            descriptor(peer, me).start()
            return carry

        lax.fori_loop(0, n - 1, start, 0)

        def finish(t, carry):
            peer = lax.rem(me + 1 + t, n)
            copy = descriptor(peer, peer)
            copy.wait_send()
            copy.wait_recv()
            return carry

        lax.fori_loop(0, n - 1, finish, 0)
        landing[me] = source(me)[...]

    barrier = pltpu.get_barrier_semaphore()

    def greet(t, carry):
        peer = lax.rem(me + 1 + t, n)
        pl.semaphore_signal(barrier, inc=1, device_id=(row, peer), device_id_type=MESH_ID)
        return carry

    lax.fori_loop(0, n - 1, greet, 0)
    pl.semaphore_wait(barrier, n - 1)
    exchange((lambda peer: send_ref) if broadcast else (lambda peer: send_ref.at[peer]), recv, send_sems, recv_sems)
    if mode == "gather":
        out_ref[...] = recv[...]
    elif mode == "scatter":
        out_ref[...] = jnp.sum(recv[...], axis=0)
    else:
        chunk, recv_back, back_send_sems, back_recv_sems = extra
        chunk[...] = jnp.sum(recv[...], axis=0)
        exchange(lambda peer: chunk, recv_back, back_send_sems, back_recv_sems)
        out_ref[...] = recv_back[...]


def col_exchange(send, n, mode, collective_id):
    piece = tuple(send.shape) if mode == "gather" else tuple(send.shape[1:])
    out_shape = piece if mode == "scatter" else (n,) + piece
    scratch = [
        pltpu.VMEM((n,) + piece, send.dtype),
        pltpu.SemaphoreType.DMA((n,)),
        pltpu.SemaphoreType.DMA((n,)),
    ]
    if mode == "allreduce":
        scratch += [
            pltpu.VMEM(piece, send.dtype),
            pltpu.VMEM((n,) + piece, send.dtype),
            pltpu.SemaphoreType.DMA((n,)),
            pltpu.SemaphoreType.DMA((n,)),
        ]
    return pl.pallas_call(
        functools.partial(_exchange_kernel, n, mode),
        out_shape=jax.ShapeDtypeStruct(out_shape, send.dtype),
        in_specs=[pl.BlockSpec(memory_space=pltpu.VMEM)],
        out_specs=pl.BlockSpec(memory_space=pltpu.VMEM),
        scratch_shapes=scratch,
        compiler_params=pltpu.CompilerParams(collective_id=collective_id, has_side_effects=True),
    )(send)


def col_gather(piece_t, n):
    gathered = col_exchange(piece_t, n, "gather", 0)
    return gathered.reshape(n * piece_t.shape[0], piece_t.shape[1]).T


def col_reduce_scatter(full, n, collective_id):
    width = full.shape[1] // n
    summed_t = col_exchange(full.T.reshape(n, width, full.shape[0]), n, "scatter", collective_id)
    return summed_t.T


def col_all_reduce(full, n, collective_id):
    width = full.shape[1] // n
    summed_t = col_exchange(full.T.reshape(n, width, full.shape[0]), n, "allreduce", collective_id)
    return summed_t.reshape(n * width, full.shape[0]).T


def local(tensor, first_factor, second_factor):
    frame_count, col_count, row_count = tensor.shape
    components = first_factor.shape[0]
    n = lax.axis_size("col")
    flattened = tensor.reshape(frame_count * col_count, row_count)
    second_values = second_factor.astype(jnp.float32)
    gram_first_part = gram_of(first_factor)
    gram_second_part = gram_of(second_factor)
    block = col_gather(first_factor.T, n)
    projected = project_columns(flattened, block)
    projected = projected.reshape(components, frame_count, col_count)
    frame_part = jnp.einsum("rkj,rj->rk", projected, second_values, precision=lax.Precision.HIGHEST)
    row_summed = lax.psum(jnp.concatenate([frame_part, gram_first_part], axis=1), "row")
    summed = col_all_reduce(jnp.concatenate([row_summed, gram_second_part], axis=1), n, 3)
    frame_sum = summed[:, :frame_count]
    gram_first = summed[:, frame_count:frame_count + components]
    gram_second = summed[:, frame_count + components:]
    frames = ridge_solve(gram_first * gram_second, frame_sum)
    gram_frames = jnp.dot(frames, frames.T, precision=lax.Precision.HIGHEST)
    weights = spread_product(frames, second_values)
    full_part = accumulate_rows(weights, flattened)
    first_sum_mine = col_reduce_scatter(full_part, n, 1)
    new_first_mine = ridge_solve(gram_second * gram_frames, first_sum_mine).astype(jnp.bfloat16)
    new_block = col_gather(new_first_mine.T, n)
    gram_new_part = gram_of(new_block)
    projected_new = project_columns(flattened, new_block)
    projected_new = projected_new.reshape(components, frame_count, col_count)
    second_part = jnp.einsum("rkj,rk->rj", projected_new, frames, precision=lax.Precision.HIGHEST)
    second_sum, gram_new = lax.psum((second_part, gram_new_part), "row")
    new_second = ridge_solve(gram_new * gram_frames, second_sum)
    weights_next = spread_product(frames, new_second)
    full_next = accumulate_rows(weights_next, flattened)
    mode_one = col_reduce_scatter(full_next, n, 2)
    return (frames, mode_one)


def solution(mesh):
    return jax.shard_map(
        local,
        mesh=mesh,
        in_specs=(P(None, "col", "row"), P(None, ("row", "col")), P(None, "col")),
        out_specs=(P(), P(None, ("row", "col"))),
        check_vma=False,
    )
```

profile of v0, /device:TPU:24, one launch (start us, length us, event | category | flops | bytes accessed | tf_op | source)
XLA Modules:
  0.0 258.6 jit_solution(17346142565888081588)
XLA Ops:
  3.4 22.6 %shard_map.50 = bf16[64,16,64]{2,1,0:T(8,128)(2,1)} custom-call(bf16[16,64]{1,0:T(8,128)(2,1)} %bitcast.92), custom_call_target="tpu_custom_call" | custom-call | tf_op jit(solution)/shard_map/pallas_call | solution.py:157
  27.7 9.9 %shard_map.51 = f32[64,6144]{1,0:T(8,128)} custom-call(bf16[64,1024]{1,0:T(8,128)(2,1)} %bitcast.86, bf16[6144,1024]{1,0:T(8,128)(2,1)} %bitcast.71), custom_call_target="tpu_custom_call" | custom-call | flops 805306368 | bytes 14155776 | tf_op jit(solution)/shard_map/pallas_call | solution.py:40
  37.6 4.5 %reshape.66 = f32[64,128,48]{2,1,0:T(8,128)} reshape(f32[64,6144]{1,0:T(8,128)} %shard_map.51) | data formatting | bytes 3145728 | tf_op jit(solution)/shard_map/reshape | solution.py:194
  42.0 3.3 %multiply_reduce_fusion = f32[64,128]{1,0:T(8,128)S(1)} fusion(f32[64,128,48]{2,1,0:T(8,128)} %reshape.66, f32[64,48]{1,0:T(8,128)S(1)} %copy.49), kind=kLoop, calls=%fused_computation | loop fusion | flops 778240 | bytes 1617920
  45.5 11.7 %psum.21 = f32[64,192]{0,1:T(8,128)S(1)} all-reduce(f32[64,192]{0,1:T(8,128)S(1)} %pad_maximum_fusion.1), channel_id=1, replica_groups=mesh['row'=4,'col'=64] {'row'}, use_global_device_ids=true, to_apply=%region_0.0 | all-reduce | flops 12288 | bytes 98304 | tf_op jit(solution)/shard_map/psum | solution.py:196
  57.8 26.8 %shard_map.52 = f32[64,4,64]{2,1,0:T(4,128)} custom-call(f32[64,4,64]{2,1,0:T(4,128)} %bitcast.88), custom_call_target="tpu_custom_call" | custom-call | tf_op jit(solution)/shard_map/pallas_call | solution.py:157
  86.0 5.9 %cholesky.59 = f32[64,64]{1,0:T(8,128)S(1)} custom-call(f32[64,64]{1,0:T(8,128)S(1)} %copy.27), custom_call_target="Cholesky" | custom-call | tf_op jit(solution)/shard_map/jit(cholesky)/cholesky | solution.py:16
  93.2 4.9 %custom-call.17 = f32[1,64,64]{1,2,0:T(8,128)S(1)} custom-call(f32[1,64,64]{2,1,0:T(8,128)S(1)} %fusion.1), custom_call_target="InvertDiagBlocksLowerTriangular" | custom-call | tf_op jit(solution)/shard_map/triangular_solve | solution.py:18
  98.9 5.9 %cholesky.70 = f32[64,64]{1,0:T(8,128)S(1)} custom-call(f32[64,64]{1,0:T(8,128)S(1)} %copy.29), custom_call_target="Cholesky" | custom-call | tf_op jit(solution)/shard_map/jit(cholesky)/cholesky | solution.py:16
  106.1 4.9 %custom-call.18 = f32[1,64,64]{1,2,0:T(8,128)S(1)} custom-call(f32[1,64,64]{2,1,0:T(8,128)S(1)} %fusion.2), custom_call_target="InvertDiagBlocksLowerTriangular" | custom-call | tf_op jit(solution)/shard_map/triangular_solve | solution.py:18
  112.4 4.8 %convert_element_type.26.weights_ref = bf16[64,6144]{1,0:T(8,128)(2,1)} reshape(bf16[64,128,48]{2,1,0:T(8,128)(2,1)S(1)} %multiply_convert_fusion.1) | data formatting | bytes 1572864 | tf_op jit(solution)/shard_map/convert_element_type | solution.py:85
  117.3 9.0 %shard_map.53 = f32[64,1024]{1,0:T(8,128)} custom-call(bf16[64,6144]{1,0:T(8,128)(2,1)} %convert_element_type.26.weights_ref, bf16[6144,1024]{1,0:T(8,128)(2,1)} %bitcast.72), custom_call_target="tpu_custom_call" | custom-call | flops 805306368 | bytes 13369344 | tf_op jit(solution)/shard_map/pallas_call | solution.py:67
  128.2 21.6 %shard_map.54 = f32[16,64]{1,0:T(8,128)} custom-call(f32[64,16,64]{2,1,0:T(8,128)} %bitcast.75), custom_call_target="tpu_custom_call" | custom-call | tf_op jit(solution)/shard_map/pallas_call | solution.py:157
  151.5 17.2 %shard_map.55 = bf16[64,16,64]{2,1,0:T(8,128)(2,1)} custom-call(bf16[16,64]{1,0:T(8,128)(2,1)} %convolution_convert_fusion.send_ref), custom_call_target="tpu_custom_call" | custom-call | tf_op jit(solution)/shard_map/pallas_call | solution.py:157
  171.7 9.9 %shard_map.56 = f32[64,6144]{1,0:T(8,128)} custom-call(bf16[64,1024]{1,0:T(8,128)(2,1)} %bitcast.87, bf16[6144,1024]{1,0:T(8,128)(2,1)} %bitcast.73), custom_call_target="tpu_custom_call" | custom-call | flops 805306368 | bytes 14155776 | tf_op jit(solution)/shard_map/pallas_call | solution.py:40
  181.6 4.5 %reshape.71 = f32[64,128,48]{2,1,0:T(8,128)} reshape(f32[64,6144]{1,0:T(8,128)} %shard_map.56) | data formatting | bytes 3145728 | tf_op jit(solution)/shard_map/reshape | solution.py:210
  186.1 5.3 %fusion.21 = f32[64,1,48]{2,1,0:T(1,128)S(1)} fusion(f32[64,128,48]{2,1,0:T(8,128)} %reshape.71, f32[64,128,1]{1,2,0:T(1,128)S(1)} %bitcast.77), kind=kOutput, calls=%fused_computation.46 | convolution fusion | flops 4718592 | bytes 1617920 | tf_op jit(solution)/shard_map/rkj,rk->rj/dot_general | solution.py:211
  191.4 11.0 %all-reduce = (f32[64,48]{1,0:T(8,128)S(1)}, f32[64,64]{1,0:T(8,128)S(1)}) all-reduce(f32[64,48]{1,0:T(8,128)S(1)} %bitcast.90, f32[64,64]{1,0:T(8,128)S(1)} %convolution_bitcast_fusion), channel_id=1, replica_groups=mesh['row'=4,'col'=64] {'row'}, use_global_device_ids=true, to_apply=%region_4.6 | all-reduce | flops 7168 | bytes 57344 | tf_op jit(solution)/shard_map/psum | solution.py:212
  202.6 5.9 %cholesky.81 = f32[64,64]{1,0:T(8,128)S(1)} custom-call(f32[64,64]{1,0:T(8,128)S(1)} %copy.35), custom_call_target="Cholesky" | custom-call | tf_op jit(solution)/shard_map/jit(cholesky)/cholesky | solution.py:16
  209.8 4.9 %custom-call.19 = f32[1,64,64]{1,2,0:T(8,128)S(1)} custom-call(f32[1,64,64]{2,1,0:T(8,128)S(1)} %fusion.3), custom_call_target="InvertDiagBlocksLowerTriangular" | custom-call | tf_op jit(solution)/shard_map/triangular_solve | solution.py:18
  216.6 4.8 %convert_element_type.29.weights_ref = bf16[64,6144]{1,0:T(8,128)(2,1)} reshape(bf16[64,128,48]{2,1,0:T(8,128)(2,1)S(1)} %multiply_convert_fusion) | data formatting | bytes 1572864 | tf_op jit(solution)/shard_map/convert_element_type | solution.py:85
  221.5 9.0 %shard_map.57 = f32[64,1024]{1,0:T(8,128)} custom-call(bf16[64,6144]{1,0:T(8,128)(2,1)} %convert_element_type.29.weights_ref, bf16[6144,1024]{1,0:T(8,128)(2,1)} %bitcast.74), custom_call_target="tpu_custom_call" | custom-call | flops 805306368 | bytes 13369344 | tf_op jit(solution)/shard_map/pallas_call | solution.py:67
  230.4 1.9 copy.38
  232.4 24.9 %shard_map.58 = f32[16,64]{1,0:T(8,128)} custom-call(f32[64,16,64]{2,1,0:T(8,128)} %bitcast.76), custom_call_target="tpu_custom_call" | custom-call | tf_op jit(solution)/shard_map/pallas_call | solution.py:157
  (43 shorter events, 22.8 us)
Async XLA Ops:
  98.5 116.7 %copy-start = (f32[64,128]{1,0:T(8,128)}, f32[64,128]{1,0:T(8,128)S(1)}, u32[]{:S(2)}) copy-start(f32[64,128]{1,0:T(8,128)S(1)} %fusion.15) | copy-start | bytes 98308
where the time goes:
time: 261 us; the launch traced here: 259 us
  Pallas kernels  151 us (58%)
  other arithmetic  43.4 us (17%)
  local copies, waits for them, and re-layouts  29.6 us (11%)
  blocking collectives  22.7 us (9%)
  matrix products  11.3 us (4%)
    pallas_call x5, Pallas kernels, col_exchange(): pl.pallas_call(functools.partial(_exchange_kernel, n, mode), out_shape=ja...  113 us
    pallas_call x2, Pallas kernels, project_columns(): pl.pallas_call(_project_kernel, grid=(cols // STREAM_ROWS,), in_specs=[pl...  19.8 us
    another operation x9, other arithmetic, ridge_solve(): jnp.linalg.cholesky(gram + ridge_weight * jnp.eye(order_size, dtype=jnp.f...  19.6 us
    pallas_call x2, Pallas kernels, accumulate_rows(): pl.pallas_call(_accumulate_kernel, grid=(cols // STREAM_ROWS,), in_specs=...  17.9 us
    another operation x6, other arithmetic, ridge_solve(): lax.linalg.triangular_solve(factor_low, middle, left_side=True, lower=Tru...  16.6 us
    psum x1, blocking collectives, local(): lax.psum(jnp.concatenate([frame_part, gram_first_part], axis=1), 'row')  11.7 us
    psum x1, blocking collectives, local(): second_sum, gram_new = lax.psum((second_part, gram_new_part), 'row')  11 us
    convert_element_type x2, local copies, waits for them, and re-layouts, spread_product(): return product.astype(jnp.bfloat16).reshape(frames.shape[0], -1)  9.64 us

commit v1 on v0

--- a/solution.py
+++ b/solution.py
@@ -118,15 +118,6 @@
         lax.fori_loop(0, n - 1, finish, 0)
         landing[me] = source(me)[...]
 
-    barrier = pltpu.get_barrier_semaphore()
-
-    def greet(t, carry):
-        peer = lax.rem(me + 1 + t, n)
-        pl.semaphore_signal(barrier, inc=1, device_id=(row, peer), device_id_type=MESH_ID)
-        return carry
-
-    lax.fori_loop(0, n - 1, greet, 0)
-    pl.semaphore_wait(barrier, n - 1)
     exchange((lambda peer: send_ref) if broadcast else (lambda peer: send_ref.at[peer]), recv, send_sems, recv_sems)
     if mode == "gather":
         out_ref[...] = recv[...]
@@ -160,7 +151,7 @@
         in_specs=[pl.BlockSpec(memory_space=pltpu.VMEM)],
         out_specs=pl.BlockSpec(memory_space=pltpu.VMEM),
         scratch_shapes=scratch,
-        compiler_params=pltpu.CompilerParams(collective_id=collective_id, has_side_effects=True),
+        compiler_params=pltpu.CompilerParams(has_side_effects=True),
     )(send)
 
 

time: 261 us -> 292 us (1.12)
  Pallas kernels: 151 us -> 182 us
    pallas_call x5, Pallas kernels: 113 us -> 145 us  [col_exchange(): pl.pallas_call(functools.partial(_exchange_kernel, n, mode), out_shape=ja...]
where the time goes in v1:
time: 292 us; the launch traced here: 289 us
  Pallas kernels  182 us (62%)
  other arithmetic  43.4 us (15%)
  local copies, waits for them, and re-layouts  29.6 us (10%)
  blocking collectives  21.9 us (8%)
  matrix products  11.3 us (4%)
    pallas_call x5, Pallas kernels, col_exchange(): pl.pallas_call(functools.partial(_exchange_kernel, n, mode), out_shape=ja...  145 us
    pallas_call x2, Pallas kernels, project_columns(): pl.pallas_call(_project_kernel, grid=(cols // STREAM_ROWS,), in_specs=[pl...  19.8 us
    another operation x9, other arithmetic, ridge_solve(): jnp.linalg.cholesky(gram + ridge_weight * jnp.eye(order_size, dtype=jnp.f...  19.6 us
    pallas_call x2, Pallas kernels, accumulate_rows(): pl.pallas_call(_accumulate_kernel, grid=(cols // STREAM_ROWS,), in_specs=...  17.9 us
    another operation x6, other arithmetic, ridge_solve(): lax.linalg.triangular_solve(factor_low, middle, left_side=True, lower=Tru...  16.6 us
    psum x1, blocking collectives, local(): lax.psum(jnp.concatenate([frame_part, gram_first_part], axis=1), 'row')  11.1 us
    psum x1, blocking collectives, local(): second_sum, gram_new = lax.psum((second_part, gram_new_part), 'row')  10.7 us
    convert_element_type x2, local copies, waits for them, and re-layouts, spread_product(): return product.astype(jnp.bfloat16).reshape(frames.shape[0], -1)  9.64 us

profile of v1, /device:TPU:24, one launch (start us, length us, event | category | flops | bytes accessed | tf_op | source)
XLA Modules:
  0.0 289.5 jit_solution(7085732783663133331)
XLA Ops:
  3.4 30.1 %shard_map.50 = bf16[64,16,64]{2,1,0:T(8,128)(2,1)} custom-call(bf16[16,64]{1,0:T(8,128)(2,1)} %bitcast.92), custom_call_target="tpu_custom_call" | custom-call | tf_op jit(solution)/shard_map/pallas_call | solution.py:148
  35.2 9.9 %shard_map.51 = f32[64,6144]{1,0:T(8,128)} custom-call(bf16[64,1024]{1,0:T(8,128)(2,1)} %bitcast.86, bf16[6144,1024]{1,0:T(8,128)(2,1)} %bitcast.71), custom_call_target="tpu_custom_call" | custom-call | flops 805306368 | bytes 14155776 | tf_op jit(solution)/shard_map/pallas_call | solution.py:40
  45.1 4.5 %reshape.66 = f32[64,128,48]{2,1,0:T(8,128)} reshape(f32[64,6144]{1,0:T(8,128)} %shard_map.51) | data formatting | bytes 3145728 | tf_op jit(solution)/shard_map/reshape | solution.py:185
  49.6 3.3 %multiply_reduce_fusion = f32[64,128]{1,0:T(8,128)S(1)} fusion(f32[64,128,48]{2,1,0:T(8,128)} %reshape.66, f32[64,48]{1,0:T(8,128)S(1)} %copy.49), kind=kLoop, calls=%fused_computation | loop fusion | flops 778240 | bytes 1617920
  53.0 11.1 %psum.21 = f32[64,192]{0,1:T(8,128)S(1)} all-reduce(f32[64,192]{0,1:T(8,128)S(1)} %pad_maximum_fusion.1), channel_id=1, replica_groups=mesh['row'=4,'col'=64] {'row'}, use_global_device_ids=true, to_apply=%region_0.0 | all-reduce | flops 12288 | bytes 98304 | tf_op jit(solution)/shard_map/psum | solution.py:187
  64.8 29.6 %shard_map.52 = f32[64,4,64]{2,1,0:T(4,128)} custom-call(f32[64,4,64]{2,1,0:T(4,128)} %bitcast.88), custom_call_target="tpu_custom_call" | custom-call | tf_op jit(solution)/shard_map/pallas_call | solution.py:148
  95.7 5.9 %cholesky.59 = f32[64,64]{1,0:T(8,128)S(1)} custom-call(f32[64,64]{1,0:T(8,128)S(1)} %copy.27), custom_call_target="Cholesky" | custom-call | tf_op jit(solution)/shard_map/jit(cholesky)/cholesky | solution.py:16
  102.9 4.9 %custom-call.17 = f32[1,64,64]{1,2,0:T(8,128)S(1)} custom-call(f32[1,64,64]{2,1,0:T(8,128)S(1)} %fusion.1), custom_call_target="InvertDiagBlocksLowerTriangular" | custom-call | tf_op jit(solution)/shard_map/triangular_solve | solution.py:18
  108.6 5.9 %cholesky.70 = f32[64,64]{1,0:T(8,128)S(1)} custom-call(f32[64,64]{1,0:T(8,128)S(1)} %copy.29), custom_call_target="Cholesky" | custom-call | tf_op jit(solution)/shard_map/jit(cholesky)/cholesky | solution.py:16
  115.8 4.9 %custom-call.18 = f32[1,64,64]{1,2,0:T(8,128)S(1)} custom-call(f32[1,64,64]{2,1,0:T(8,128)S(1)} %fusion.2), custom_call_target="InvertDiagBlocksLowerTriangular" | custom-call | tf_op jit(solution)/shard_map/triangular_solve | solution.py:18
  122.2 4.8 %convert_element_type.26.weights_ref = bf16[64,6144]{1,0:T(8,128)(2,1)} reshape(bf16[64,128,48]{2,1,0:T(8,128)(2,1)S(1)} %multiply_convert_fusion.1) | data formatting | bytes 1572864 | tf_op jit(solution)/shard_map/convert_element_type | solution.py:85
  127.0 9.0 %shard_map.53 = f32[64,1024]{1,0:T(8,128)} custom-call(bf16[64,6144]{1,0:T(8,128)(2,1)} %convert_element_type.26.weights_ref, bf16[6144,1024]{1,0:T(8,128)(2,1)} %bitcast.72), custom_call_target="tpu_custom_call" | custom-call | flops 805306368 | bytes 13369344 | tf_op jit(solution)/shard_map/pallas_call | solution.py:67
  136.0 1.9 copy.31
  137.9 32.3 %shard_map.54 = f32[16,64]{1,0:T(8,128)} custom-call(f32[64,16,64]{2,1,0:T(8,128)} %bitcast.75), custom_call_target="tpu_custom_call" | custom-call | tf_op jit(solution)/shard_map/pallas_call | solution.py:148
  172.0 23.5 %shard_map.55 = bf16[64,16,64]{2,1,0:T(8,128)(2,1)} custom-call(bf16[16,64]{1,0:T(8,128)(2,1)} %convolution_convert_fusion.send_ref), custom_call_target="tpu_custom_call" | custom-call | tf_op jit(solution)/shard_map/pallas_call | solution.py:148
  198.5 9.9 %shard_map.56 = f32[64,6144]{1,0:T(8,128)} custom-call(bf16[64,1024]{1,0:T(8,128)(2,1)} %bitcast.87, bf16[6144,1024]{1,0:T(8,128)(2,1)} %bitcast.73), custom_call_target="tpu_custom_call" | custom-call | flops 805306368 | bytes 14155776 | tf_op jit(solution)/shard_map/pallas_call | solution.py:40
  208.4 4.5 %reshape.71 = f32[64,128,48]{2,1,0:T(8,128)} reshape(f32[64,6144]{1,0:T(8,128)} %shard_map.56) | data formatting | bytes 3145728 | tf_op jit(solution)/shard_map/reshape | solution.py:201
  212.9 5.3 %fusion.21 = f32[64,1,48]{2,1,0:T(1,128)S(1)} fusion(f32[64,128,48]{2,1,0:T(8,128)} %reshape.71, f32[64,128,1]{1,2,0:T(1,128)S(1)} %bitcast.77), kind=kOutput, calls=%fused_computation.46 | convolution fusion | flops 4718592 | bytes 1617920 | tf_op jit(solution)/shard_map/rkj,rk->rj/dot_general | solution.py:202
  218.2 10.7 %all-reduce = (f32[64,48]{1,0:T(8,128)S(1)}, f32[64,64]{1,0:T(8,128)S(1)}) all-reduce(f32[64,48]{1,0:T(8,128)S(1)} %bitcast.90, f32[64,64]{1,0:T(8,128)S(1)} %convolution_bitcast_fusion), channel_id=1, replica_groups=mesh['row'=4,'col'=64] {'row'}, use_global_device_ids=true, to_apply=%region_4.6 | all-reduce | flops 7168 | bytes 57344 | tf_op jit(solution)/shard_map/psum | solution.py:203
  229.2 5.9 %cholesky.81 = f32[64,64]{1,0:T(8,128)S(1)} custom-call(f32[64,64]{1,0:T(8,128)S(1)} %copy.35), custom_call_target="Cholesky" | custom-call | tf_op jit(solution)/shard_map/jit(cholesky)/cholesky | solution.py:16
  236.4 4.9 %custom-call.19 = f32[1,64,64]{1,2,0:T(8,128)S(1)} custom-call(f32[1,64,64]{2,1,0:T(8,128)S(1)} %fusion.3), custom_call_target="InvertDiagBlocksLowerTriangular" | custom-call | tf_op jit(solution)/shard_map/triangular_solve | solution.py:18
  243.2 4.8 %convert_element_type.29.weights_ref = bf16[64,6144]{1,0:T(8,128)(2,1)} reshape(bf16[64,128,48]{2,1,0:T(8,128)(2,1)S(1)} %multiply_convert_fusion) | data formatting | bytes 1572864 | tf_op jit(solution)/shard_map/convert_element_type | solution.py:85
  248.0 9.0 %shard_map.57 = f32[64,1024]{1,0:T(8,128)} custom-call(bf16[64,6144]{1,0:T(8,128)(2,1)} %convert_element_type.29.weights_ref, bf16[6144,1024]{1,0:T(8,128)(2,1)} %bitcast.74), custom_call_target="tpu_custom_call" | custom-call | flops 805306368 | bytes 13369344 | tf_op jit(solution)/shard_map/pallas_call | solution.py:67
  258.9 29.2 %shard_map.58 = f32[16,64]{1,0:T(8,128)} custom-call(f32[64,16,64]{2,1,0:T(8,128)} %bitcast.76), custom_call_target="tpu_custom_call" | custom-call | tf_op jit(solution)/shard_map/pallas_call | solution.py:148
  (43 shorter events, 22.8 us)
Async XLA Ops:
  108.3 133.4 %copy-start = (f32[64,128]{1,0:T(8,128)}, f32[64,128]{1,0:T(8,128)S(1)}, u32[]{:S(2)}) copy-start(f32[64,128]{1,0:T(8,128)S(1)} %fusion.15) | copy-start | bytes 98308
